TPU v7x, 32 devices: a whole 2x2x4 slice. The times are simulated.
32 devices in a mesh: shard: 4 (over y, x), rep: 8 (over z, core).
Axes of the slice: x: 2, y: 2, z: 4, core: 2. Of those that a mesh axis runs over, the one named last changes fastest.
Arguments:
- tokens: bfloat16 [32768, 1024], P(('shard', 'rep')), may hold values from -6 to 6
- cotangent: bfloat16 [32768, 1024], P(('shard', 'rep')), may hold values from -6 to 6
- segment: int32 [32768], P(('shard', 'rep')), may hold values from -1 to 15, as said below
- attn_gain: bfloat16 [1024], P('shard'), may hold values from 0.5 to 1.5
- w_query: bfloat16 [1024, 1024], P('shard'), may hold values from -0.1875 to 0.1875
- w_key: bfloat16 [1024, 512], P('shard'), may hold values from -0.1875 to 0.1875
- w_value: bfloat16 [1024, 512], P('shard'), may hold values from -0.1875 to 0.1875
- qk_gain: bfloat16 [128], P('shard'), may hold values from 0.099609375 to 1.8984375
- w_out: bfloat16 [1024, 1024], P('shard'), may hold values from -1.5 to 1.5
- ffn_gain: bfloat16 [1024], P('shard'), may hold values from 0.5 to 1.5
- w_gate: bfloat16 [1024, 4608], P('shard'), may hold values from -0.1875 to 0.1875
- w_up: bfloat16 [1024, 4608], P('shard'), may hold values from -0.1875 to 0.1875
- w_down: bfloat16 [4608, 1024], P('shard'), may hold values from -0.09375 to 0.09375
Outputs:
- out: bfloat16 [32768, 1024], P(('shard', 'rep'))
- grad_tokens: bfloat16 [32768, 1024], P(('shard', 'rep'))
- grad_attn_gain: float32 [1024], P('shard')
- grad_w_query: float32 [1024, 1024], P('shard')
- grad_w_key: float32 [1024, 512], P('shard')
- grad_w_value: float32 [1024, 512], P('shard')
- grad_qk_gain: float32 [128], P('shard')
- grad_w_out: float32 [1024, 1024], P('shard')
- grad_ffn_gain: float32 [1024], P('shard')
- grad_w_gate: float32 [1024, 4608], P('shard')
- grad_w_up: float32 [1024, 4608], P('shard')
- grad_w_down: float32 [4608, 1024], P('shard')
Inputs may be any that keep to these rules, and one draw needn't show every extreme that they name: `segment`: within each device's 1024 slots the live tokens come first, 512 to 1024 of them, followed by padding marked -1; live tokens form runs of equal ids 0, 1, 2, ... in rising order, each run one sequence of 1 to 512 tokens, at most 16 of them on a device. Some device has no padding and holds 16 sequences, some has 512 live tokens, and some sequence has exactly 512 tokens.
All inputs are finite; a program needn't handle non-finite values.
Results may differ from a plain program's by a relative error of at most 0.02.
Values may be sent and summed in bfloat16 or wider, within the bound.
No kernel may reach another device: no remote copies, remote signals or barrier semaphores. Data moves between devices by JAX's collectives and lax.ppermute only.
A program may use at most 384 MiB of HBM per device.

v0:
```python
import math
import jax
import jax.numpy as jnp
from jax import lax
from jax.sharding import PartitionSpec as P

HQ = 16
HK = 8
HD = 64
norm_eps = 1e-05
rope_base = 1000000.0


def inv_rms(values):
    return lax.rsqrt(jnp.mean(values * values, axis=-1, keepdims=True) + norm_eps)


def rope_tables(positions):
    half_dim = HD // 2
    freq_index = jnp.arange(half_dim).astype(jnp.float32)
    freq_vals = jnp.power(rope_base, -(2.0 * freq_index) / HD)
    angles = positions[:, None] * freq_vals[None, :]
    return (jnp.cos(angles)[:, None, :], jnp.sin(angles)[:, None, :])


def rotate(values, cosine, sine_table):
    half_dim = HD // 2
    first_half = values[..., :half_dim]
    second_half = values[..., half_dim:]
    return jnp.concatenate(
        [
            first_half * cosine - second_half * sine_table,
            second_half * cosine + first_half * sine_table,
        ],
        axis=-1,
    )


def rotate_back(grad_vals, cosine, sine_table):
    half_dim = HD // 2
    first_half = grad_vals[..., :half_dim]
    second_half = grad_vals[..., half_dim:]
    return jnp.concatenate(
        [
            first_half * cosine + second_half * sine_table,
            second_half * cosine - first_half * sine_table,
        ],
        axis=-1,
    )


def norm_back(grad_out, inputs, scale_inv, gain_vec):
    weighted = grad_out * gain_vec
    row_inner = jnp.mean(weighted * inputs, axis=-1, keepdims=True)
    return scale_inv * weighted - inputs * (scale_inv * scale_inv * scale_inv) * row_inner


def matmul_plain(left_mat, right_mat):
    return jnp.dot(left_mat, right_mat, preferred_element_type=jnp.float32)


def matmul_rows(left_mat, right_mat):
    return lax.dot_general(
        left_mat, right_mat, (((0,), (0,)), ((), ())), preferred_element_type=jnp.float32
    )


def matmul_cols(left_mat, right_mat):
    return lax.dot_general(
        left_mat, right_mat, (((1,), (1,)), ((), ())), preferred_element_type=jnp.float32
    )


def body(
    tokens,
    cotangent,
    segment,
    attn_gain,
    w_query,
    w_key,
    w_value,
    qk_gain,
    w_out,
    ffn_gain,
    w_gate,
    w_up,
    w_down,
):
    row_count = tokens.shape[0]
    group_size = HQ // HK
    score_scale = 1.0 / math.sqrt(HD)
    block_rows = min(512, row_count)
    block_count = row_count // block_rows
    attn_set = (
        lax.all_gather(attn_gain, "shard", axis=0, tiled=True),
        lax.all_gather(w_query, "shard", axis=0, tiled=True),
        lax.all_gather(w_key, "shard", axis=0, tiled=True),
        lax.all_gather(w_value, "shard", axis=0, tiled=True),
        lax.all_gather(qk_gain, "shard", axis=0, tiled=True),
        lax.all_gather(w_out, "shard", axis=0, tiled=True),
    )
    full_attn_gain, full_query, full_key, full_value, full_qk_gain, full_out = attn_set
    inputs = tokens.astype(jnp.float32)
    token_index = jnp.arange(row_count)
    same_seq = segment[:, None] == segment[None, :]
    allowed = same_seq & (token_index[None, :] <= token_index[:, None])
    positions = jnp.sum(
        (same_seq & (token_index[None, :] < token_index[:, None])).astype(jnp.float32), axis=1
    )
    live_rows = (segment >= 0).astype(jnp.float32)[:, None]
    cosine, sine_table = rope_tables(positions)
    scale_one = inv_rms(inputs)
    normed = (inputs * scale_one * full_attn_gain.astype(jnp.float32)).astype(jnp.bfloat16)
    query_lin = matmul_plain(normed, full_query).reshape(row_count, HQ, HD)
    key_lin = matmul_plain(normed, full_key).reshape(row_count, HK, HD)
    value_low = matmul_plain(normed, full_value).astype(jnp.bfloat16).reshape(row_count, HK, HD)
    qk_gains = full_qk_gain.astype(jnp.float32)
    query_scale = inv_rms(query_lin)
    key_scale = inv_rms(key_lin)
    query_rot = (
        rotate(query_lin * query_scale * qk_gains[:HD], cosine, sine_table)
        .astype(jnp.bfloat16)
        .reshape(row_count, HK, group_size, HD)
    )
    key_rot = rotate(key_lin * key_scale * qk_gains[HD:], cosine, sine_table).astype(jnp.bfloat16)

    def block_scores(begin_row):
        query_block = query_rot[begin_row : begin_row + block_rows]
        raw_scores = score_scale * jnp.einsum(
            "qgrd,kgd->grqk", query_block, key_rot, preferred_element_type=jnp.float32
        )
        mask_block = allowed[begin_row : begin_row + block_rows]
        return jnp.where(mask_block[None, None, :, :], raw_scores, -1e30)

    lse_parts = []
    attended_parts = []
    for block_id in range(block_count):
        begin_row = block_id * block_rows
        masked = block_scores(begin_row)
        row_peak = jnp.max(masked, axis=-1, keepdims=True)
        exp_scores = jnp.exp(masked - row_peak)
        row_total = jnp.sum(exp_scores, axis=-1, keepdims=True)
        probs_low = (exp_scores / row_total).astype(jnp.bfloat16)
        lse_parts.append(row_peak + jnp.log(row_total))
        attended_parts.append(
            jnp.einsum("grqk,kgd->qgrd", probs_low, value_low, preferred_element_type=jnp.float32)
        )
    attn_low = (
        jnp.concatenate(attended_parts, axis=0).astype(jnp.bfloat16).reshape(row_count, HQ * HD)
    )
    hidden = inputs + matmul_plain(attn_low, full_out)
    ffn_set = (
        lax.all_gather(ffn_gain, "shard", axis=0, tiled=True),
        lax.all_gather(w_gate, "shard", axis=0, tiled=True),
        lax.all_gather(w_up, "shard", axis=0, tiled=True),
        lax.all_gather(w_down, "shard", axis=0, tiled=True),
    )
    full_ffn_gain, full_gate, full_up, full_down = ffn_set
    scale_two = inv_rms(hidden)
    normed_ffn = (hidden * scale_two * full_ffn_gain.astype(jnp.float32)).astype(jnp.bfloat16)
    gate_proj = matmul_plain(normed_ffn, full_gate)
    up_proj = matmul_plain(normed_ffn, full_up)
    gate_sig = jax.nn.sigmoid(gate_proj)
    gate_act = gate_proj * gate_sig
    mixed_act = (gate_act * up_proj).astype(jnp.bfloat16)
    result = live_rows * (hidden + matmul_plain(mixed_act, full_down))
    back_ffn = (
        lax.all_gather(ffn_gain, "shard", axis=0, tiled=True),
        lax.all_gather(w_gate, "shard", axis=0, tiled=True),
        lax.all_gather(w_up, "shard", axis=0, tiled=True),
        lax.all_gather(w_down, "shard", axis=0, tiled=True),
    )
    back_ffn_gain, back_gate, back_up, back_down = back_ffn
    out_grad = live_rows * cotangent.astype(jnp.float32)
    out_low = out_grad.astype(jnp.bfloat16)
    grad_mixed = matmul_cols(out_low, back_down)
    grad_w_down = matmul_rows(mixed_act, out_low)
    grad_up_low = (grad_mixed * gate_act).astype(jnp.bfloat16)
    grad_gate_low = (grad_mixed * up_proj * gate_sig * (1.0 + gate_proj * (1.0 - gate_sig))).astype(
        jnp.bfloat16
    )
    grad_w_gate = matmul_rows(normed_ffn, grad_gate_low)
    grad_w_up = matmul_rows(normed_ffn, grad_up_low)
    grad_normed_ffn = matmul_cols(grad_gate_low, back_gate) + matmul_cols(grad_up_low, back_up)
    grad_ffn_gain = jnp.sum(grad_normed_ffn * hidden * scale_two, axis=0)
    grad_hidden = out_grad + norm_back(
        grad_normed_ffn, hidden, scale_two, back_ffn_gain.astype(jnp.float32)
    )
    share_fgain, share_gate, share_up, share_down = (
        lax.psum_scatter(
            grad_ffn_gain.astype(jnp.bfloat16), "shard", scatter_dimension=0, tiled=True
        ).astype(jnp.float32),
        lax.psum_scatter(
            grad_w_gate.astype(jnp.bfloat16), "shard", scatter_dimension=0, tiled=True
        ).astype(jnp.float32),
        lax.psum_scatter(
            grad_w_up.astype(jnp.bfloat16), "shard", scatter_dimension=0, tiled=True
        ).astype(jnp.float32),
        lax.psum_scatter(
            grad_w_down.astype(jnp.bfloat16), "shard", scatter_dimension=0, tiled=True
        ).astype(jnp.float32),
    )
    back_attn = (
        lax.all_gather(attn_gain, "shard", axis=0, tiled=True),
        lax.all_gather(w_query, "shard", axis=0, tiled=True),
        lax.all_gather(w_key, "shard", axis=0, tiled=True),
        lax.all_gather(w_value, "shard", axis=0, tiled=True),
        lax.all_gather(qk_gain, "shard", axis=0, tiled=True),
        lax.all_gather(w_out, "shard", axis=0, tiled=True),
    )
    back_attn_gain, back_query, back_key, back_value, back_qk_gain, back_out = back_attn
    hidden_low = grad_hidden.astype(jnp.bfloat16)
    grad_attn_low = (
        matmul_cols(hidden_low, back_out)
        .astype(jnp.bfloat16)
        .reshape(row_count, HK, group_size, HD)
    )
    grad_w_out = matmul_rows(attn_low, hidden_low)
    grad_query_parts = []
    grad_key_rot = jnp.zeros((row_count, HK, HD), jnp.float32)
    grad_value = jnp.zeros((row_count, HK, HD), jnp.float32)
    for block_id in range(block_count):
        begin_row = block_id * block_rows
        masked = block_scores(begin_row)
        attn_probs = jnp.exp(masked - lse_parts[block_id])
        probs_low = attn_probs.astype(jnp.bfloat16)
        grad_block = grad_attn_low[begin_row : begin_row + block_rows]
        query_block = query_rot[begin_row : begin_row + block_rows]
        grad_probs = jnp.einsum(
            "qgrd,kgd->grqk", grad_block, value_low, preferred_element_type=jnp.float32
        )
        row_inner = jnp.sum(attn_probs * grad_probs, axis=-1, keepdims=True)
        grad_scores = (attn_probs * (grad_probs - row_inner)).astype(jnp.bfloat16)
        grad_query_parts.append(
            score_scale
            * jnp.einsum("grqk,kgd->qgrd", grad_scores, key_rot, preferred_element_type=jnp.float32)
        )
        grad_key_rot = grad_key_rot + score_scale * jnp.einsum(
            "grqk,qgrd->kgd", grad_scores, query_block, preferred_element_type=jnp.float32
        )
        grad_value = grad_value + jnp.einsum(
            "grqk,qgrd->kgd", probs_low, grad_block, preferred_element_type=jnp.float32
        )
    grad_query_rot = jnp.concatenate(grad_query_parts, axis=0).reshape(row_count, HQ, HD)
    grad_query_norm = rotate_back(grad_query_rot, cosine, sine_table)
    grad_key_norm = rotate_back(grad_key_rot, cosine, sine_table)
    back_gains = back_qk_gain.astype(jnp.float32)
    grad_qk_gain = jnp.concatenate(
        [
            jnp.sum(grad_query_norm * query_lin * query_scale, axis=(0, 1)),
            jnp.sum(grad_key_norm * key_lin * key_scale, axis=(0, 1)),
        ]
    )
    grad_query_low = (
        norm_back(grad_query_norm, query_lin, query_scale, back_gains[:HD])
        .astype(jnp.bfloat16)
        .reshape(row_count, HQ * HD)
    )
    grad_key_low = (
        norm_back(grad_key_norm, key_lin, key_scale, back_gains[HD:])
        .astype(jnp.bfloat16)
        .reshape(row_count, HK * HD)
    )
    grad_value_low = grad_value.astype(jnp.bfloat16).reshape(row_count, HK * HD)
    grad_w_query = matmul_rows(normed, grad_query_low)
    grad_w_key = matmul_rows(normed, grad_key_low)
    grad_w_value = matmul_rows(normed, grad_value_low)
    grad_normed = (
        matmul_cols(grad_query_low, back_query)
        + matmul_cols(grad_key_low, back_key)
        + matmul_cols(grad_value_low, back_value)
    )
    grad_attn_gain = jnp.sum(grad_normed * inputs * scale_one, axis=0)
    grad_inputs = grad_hidden + norm_back(
        grad_normed, inputs, scale_one, back_attn_gain.astype(jnp.float32)
    )
    share_again, share_query, share_key, share_value, share_qk, share_out = (
        lax.psum_scatter(
            grad_attn_gain.astype(jnp.bfloat16), "shard", scatter_dimension=0, tiled=True
        ).astype(jnp.float32),
        lax.psum_scatter(
            grad_w_query.astype(jnp.bfloat16), "shard", scatter_dimension=0, tiled=True
        ).astype(jnp.float32),
        lax.psum_scatter(
            grad_w_key.astype(jnp.bfloat16), "shard", scatter_dimension=0, tiled=True
        ).astype(jnp.float32),
        lax.psum_scatter(
            grad_w_value.astype(jnp.bfloat16), "shard", scatter_dimension=0, tiled=True
        ).astype(jnp.float32),
        lax.psum_scatter(
            grad_qk_gain.astype(jnp.bfloat16), "shard", scatter_dimension=0, tiled=True
        ).astype(jnp.float32),
        lax.psum_scatter(
            grad_w_out.astype(jnp.bfloat16), "shard", scatter_dimension=0, tiled=True
        ).astype(jnp.float32),
    )
    (
        share_again,
        share_query,
        share_key,
        share_value,
        share_qk,
        share_out,
        share_fgain,
        share_gate,
        share_up,
        share_down,
    ) = (
        lax.psum(share_again.astype(jnp.bfloat16), "rep").astype(jnp.float32),
        lax.psum(share_query.astype(jnp.bfloat16), "rep").astype(jnp.float32),
        lax.psum(share_key.astype(jnp.bfloat16), "rep").astype(jnp.float32),
        lax.psum(share_value.astype(jnp.bfloat16), "rep").astype(jnp.float32),
        lax.psum(share_qk.astype(jnp.bfloat16), "rep").astype(jnp.float32),
        lax.psum(share_out.astype(jnp.bfloat16), "rep").astype(jnp.float32),
        lax.psum(share_fgain.astype(jnp.bfloat16), "rep").astype(jnp.float32),
        lax.psum(share_gate.astype(jnp.bfloat16), "rep").astype(jnp.float32),
        lax.psum(share_up.astype(jnp.bfloat16), "rep").astype(jnp.float32),
        lax.psum(share_down.astype(jnp.bfloat16), "rep").astype(jnp.float32),
    )
    return (
        result.astype(jnp.bfloat16),
        grad_inputs.astype(jnp.bfloat16),
        share_again,
        share_query,
        share_key,
        share_value,
        share_qk,
        share_out,
        share_fgain,
        share_gate,
        share_up,
        share_down,
    )


def solution(mesh):
    return jax.shard_map(
        body,
        mesh=mesh,
        in_specs=(
            P(("shard", "rep"), None),
            P(("shard", "rep"), None),
            P(("shard", "rep")),
            P("shard"),
            P("shard", None),
            P("shard", None),
            P("shard", None),
            P("shard"),
            P("shard", None),
            P("shard"),
            P("shard", None),
            P("shard", None),
            P("shard", None),
        ),
        out_specs=(
            P(("shard", "rep"), None),
            P(("shard", "rep"), None),
            P("shard"),
            P("shard", None),
            P("shard", None),
            P("shard", None),
            P("shard"),
            P("shard", None),
            P("shard"),
            P("shard", None),
            P("shard", None),
            P("shard", None),
        ),
        check_vma=False,
    )
```

profile of v0, /device:TPU:0, one launch (start us, length us, event | category | flops | bytes accessed | tf_op | source)
XLA Modules:
  0.0 1275.4 jit_solution(9859009708675031357)
XLA Ops:
  71.4 33.6 %all-gather.14.cloned.1.call-done = bf16[1024,1024]{1,0:T(8,128)(2,1)} async-done(((bf16[256,1024]{1,0:T(8,128)(2,1)}), bf16[1024,1024]{1,0:T(8,128)(2,1)}) %all-gather.14.cloned.1.call-update) | async-done | bytes 2097168 | tf_op jit(solution)/shard_map/all_gather | solution.py:96
  181.5 16.7 %fusion.45 = bf16[8,64,2,512]{3,1,2,0:T(8,128)(2,1)} fusion(bf16[1024,8,64,1]{0,2,3,1:T(8,128)(2,1)S(1)} %bitcast.201, f32[8,2,512,1024]{2,3,1,0:T(8,128)} %get-tuple-element.111, f32[8,2,512]{2,1,0:T(2,128)S(1)} %fusion.6, f32[8,2,512]{2,1,0:T(2,128)S(1)} %get-tuple-element.110), kind=kOutput, calls=%fused_computation.116 | convolution fusion | flops 1099431936 | bytes 35717120 | tf_op jit(solution)/shard_map/grqk,kgd->qgrd/dot_general | solution.py:146
  205.5 34.6 %all-gather.20.cloned.1.call-done = bf16[1024,4608]{1,0:T(8,128)(2,1)} async-done(((bf16[256,4608]{1,0:T(8,128)(2,1)}), bf16[1024,4608]{1,0:T(8,128)(2,1)}) %all-gather.20.cloned.1.call-update) | async-done | bytes 9437200 | tf_op jit(solution)/shard_map/all_gather | solution.py:155
  240.1 16.2 %fusion.66 = f32[1024,4608]{1,0:T(8,128)} fusion(bf16[1024,1024]{0,1:T(8,128)(2,1)S(1)} %multiply_convert_fusion.4, bf16[1024,4608]{1,0:T(8,128)(2,1)} %all-gather.20.cloned.1.call-done), kind=kOutput, calls=%fused_computation.156 | convolution fusion | flops 9663676416 | bytes 30408704 | tf_op jit(solution)/shard_map/dot_general | solution.py:59
  256.3 81.8 %all-gather.18.cloned.1.call-done = bf16[1024,4608]{1,0:T(8,128)(2,1)} async-done(((bf16[256,4608]{1,0:T(8,128)(2,1)}), bf16[1024,4608]{1,0:T(8,128)(2,1)}) %all-gather.18.cloned.1.call-update) | async-done | bytes 9437200 | tf_op jit(solution)/shard_map/all_gather | solution.py:154
  338.2 17.1 %fusion.65 = f32[1024,4608]{1,0:T(8,128)} fusion(bf16[1024,1024]{0,1:T(8,128)(2,1)} %copy-done.31, bf16[1024,4608]{1,0:T(8,128)(2,1)} %all-gather.18.cloned.1.call-done), kind=kOutput, calls=%fused_computation.155 | convolution fusion | flops 9663676416 | bytes 30408704 | tf_op jit(solution)/shard_map/dot_general | solution.py:59
  355.2 81.1 %all-gather.22.cloned.1.call-done = bf16[4608,1024]{1,0:T(8,128)(2,1)} async-done(((bf16[1152,1024]{1,0:T(8,128)(2,1)}), bf16[4608,1024]{1,0:T(8,128)(2,1)}) %all-gather.22.cloned.1.call-update) | async-done | bytes 9437200 | tf_op jit(solution)/shard_map/all_gather | solution.py:156
  436.4 31.2 %multiply_convert_fusion = (bf16[1024,4608]{1,0:T(8,128)(2,1)}, bf16[1024,4608]{1,0:T(8,128)(2,1)}, bf16[1024,4608]{1,0:T(8,128)(2,1)}) fusion(f32[1024,4608]{1,0:T(8,128)} %fusion.65, f32[1024,4608]{1,0:T(8,128)} %fusion.66, bf16[4608,1024]{1,0:T(8,128)(2,1)} %all-gather.22.cloned.1.call-done, bf16[1024,1024]{0,1:T(8,128)(2,1)S(1)} %copy-done.18, ...), kind=kOutput, calls=%fused_computation.22 | convolution fusion | flops 9737601024 | bytes 77598720 | tf_op jit(solution)/shard_map/dot_general | solution.py:69
  482.2 16.5 %multiply_reduce_fusion = (bf16[1024]{0:T(1024)(128)(2,1)}, f32[1024]{0:T(1024)S(1)}, f32[1024,1024]{0,1:T(8,128)S(1)}) fusion(f32[1024,1024]{0,1:T(8,128)S(1)} %copy-done.9, f32[1024]{0:T(1024)S(1)} %get-tuple-element.99, f32[1024]{0:T(1024)S(1)} %bitcast.223, f32[1024,1024]{0,1:T(8,128)S(1)} %fusion.67, bf16[1024,4608]{1,0:T(8,128)(2,1)} %get-tuple-element.65, ...), kind=kOutput, calls=%fused_computation.65 | convolution fusion | flops 9671014400 | bytes 31471616 | tf_op jit(solution)/shard_map/dot_general | solution.py:69
  517.5 21.8 %fusion = (f32[8,2,512]{2,1,0:T(2,128)S(1)}, f32[8,1024,512,2]{2,1,3,0:T(8,128)}) fusion(f32[8,2,512,1024]{2,3,1,0:T(8,128)} %get-tuple-element.109, f32[8,2,512]{2,1,0:T(2,128)S(1)} %bitcast.205, bf16[1024,8,64,1]{0,2,3,1:T(8,128)(2,1)S(1)} %bitcast.202, bf16[512,8,2,64]{0,3,2,1:T(8,128)(2,1)S(1)} %bitcast.193), kind=kOutput, calls=%fused_computation.2 | convolution fusion | flops 1098899456 | bytes 69271552 | tf_op jit(solution)/shard_map/qgrd,kgd->grqk/dot_general | solution.py:229
  539.3 21.7 %fusion.3 = (f32[8,2,512]{2,1,0:T(2,128)S(1)}, f32[8,1024,512,2]{2,1,3,0:T(8,128)}) fusion(f32[8,2,512,1024]{2,3,1,0:T(8,128)} %get-tuple-element.111, f32[8,2,512]{2,1,0:T(2,128)S(1)} %bitcast.207, bf16[1024,8,64,1]{0,2,3,1:T(8,128)(2,1)S(1)} %bitcast.203, bf16[512,8,2,64]{0,3,2,1:T(8,128)(2,1)S(1)} %bitcast.190), kind=kOutput, calls=%fused_computation.7 | convolution fusion | flops 1098899456 | bytes 69271552 | tf_op jit(solution)/shard_map/qgrd,kgd->grqk/dot_general | solution.py:229
  561.0 15.3 %fusion.36 = bf16[8,64,1024]{2,1,0:T(8,128)(2,1)} fusion(f32[8,64,1024,1]{2,1,3,0:T(8,128)} %fusion.11, bf16[512,8,2,64]{0,3,2,1:T(8,128)(2,1)S(1)} %bitcast.191, f32[8,2,512,1024]{2,3,1,0:T(8,128)} %get-tuple-element.111, f32[8,2,512]{2,1,0:T(2,128)S(1)} %bitcast.208), kind=kOutput, calls=%fused_computation.90 | convolution fusion | flops 1091567616 | bytes 37781504 | tf_op jit(solution)/shard_map/grqk,qgrd->kgd/dot_general | solution.py:241
  580.0 28.0 %fusion.5 = bf16[8,2,512,1024]{2,3,1,0:T(8,128)(2,1)} fusion(f32[8,1024,512,2]{2,1,3,0:T(8,128)} %get-tuple-element.118, f32[8,2,512,1024]{2,3,1,0:T(8,128)} %get-tuple-element.111, f32[8,2,512]{2,1,0:T(2,128)S(1)} %get-tuple-element.117, f32[8,2,512]{2,1,0:T(2,128)S(1)} %bitcast.209), kind=kLoop, calls=%fused_computation.9 | loop fusion | flops 33554432 | bytes 83951616 | tf_op jit(solution)/shard_map/convert_element_type | solution.py:233
  620.2 27.5 %fusion.2 = bf16[8,2,512,1024]{2,3,1,0:T(8,128)(2,1)} fusion(f32[8,1024,512,2]{2,1,3,0:T(8,128)} %get-tuple-element.116, f32[8,2,512,1024]{2,3,1,0:T(8,128)} %get-tuple-element.109, f32[8,2,512]{2,1,0:T(2,128)S(1)} %get-tuple-element.115, f32[8,2,512]{2,1,0:T(2,128)S(1)} %bitcast.206), kind=kLoop, calls=%fused_computation.4 | loop fusion | flops 33554432 | bytes 83951616 | tf_op jit(solution)/shard_map/convert_element_type | solution.py:233
  702.9 16.7 %convolution_convert_fusion.1 = bf16[1024,4608]{1,0:T(8,128)(2,1)} fusion(bf16[1024,1024]{0,1:T(8,128)(2,1)} %copy-done.31, bf16[1024,4608]{1,0:T(8,128)(2,1)} %get-tuple-element.66), kind=kOutput, calls=%fused_computation.34 | convolution fusion | flops 9668395008 | bytes 20971520 | tf_op jit(solution)/shard_map/dot_general | solution.py:63
  719.7 16.3 %convolution_convert_fusion = bf16[1024,4608]{1,0:T(8,128)(2,1)} fusion(bf16[1024,1024]{0,1:T(8,128)(2,1)} %copy-done.31, bf16[1024,4608]{1,0:T(8,128)(2,1)} %get-tuple-element.65), kind=kOutput, calls=%fused_computation.33 | convolution fusion | flops 9668395008 | bytes 20971520 | tf_op jit(solution)/shard_map/dot_general | solution.py:63
  736.6 16.6 %convolution_convert_fusion.2 = bf16[4608,1024]{1,0:T(8,128)(2,1)} fusion(bf16[1024,4608]{1,0:T(8,128)(2,1)} %get-tuple-element.67, bf16[1024,1024]{0,1:T(8,128)(2,1)} %copy.65, f32[1024]{0:T(1024)S(1)} %copy-done.52), kind=kOutput, calls=%fused_computation.35 | convolution fusion | flops 9671540736 | bytes 20975616 | tf_op jit(solution)/shard_map/dot_general | solution.py:63
  754.8 17.3 %reduce-scatter.8.cloned.1.call-done = bf16[256,1024]{1,0:T(8,128)(2,1)} async-done(((bf16[1024,1024]{1,0:T(8,128)(2,1)}), bf16[256,1024]{1,0:T(8,128)(2,1)}) %reduce-scatter.8.cloned.1.call-update) | async-done | bytes 524304 | tf_op jit(solution)/shard_map/reduce_scatter | solution.py:281
  772.1 98.0 %reduce-scatter.16.cloned.1.call-done = bf16[256,4608]{1,0:T(8,128)(2,1)} async-done(((bf16[1024,4608]{1,0:T(8,128)(2,1)}), bf16[256,4608]{1,0:T(8,128)(2,1)}) %reduce-scatter.16.cloned.1.call-update) | async-done | bytes 2359312 | tf_op jit(solution)/shard_map/reduce_scatter | solution.py:193
  870.2 98.1 %reduce-scatter.18.cloned.1.call-done = bf16[256,4608]{1,0:T(8,128)(2,1)} async-done(((bf16[1024,4608]{1,0:T(8,128)(2,1)}), bf16[256,4608]{1,0:T(8,128)(2,1)}) %reduce-scatter.18.cloned.1.call-update) | async-done | bytes 2359312 | tf_op jit(solution)/shard_map/reduce_scatter | solution.py:196
  968.3 98.0 %reduce-scatter.20.cloned.1.call-done = bf16[1152,1024]{1,0:T(8,128)(2,1)} async-done(((bf16[4608,1024]{1,0:T(8,128)(2,1)}), bf16[1152,1024]{1,0:T(8,128)(2,1)}) %reduce-scatter.20.cloned.1.call-update) | async-done | bytes 2359312 | tf_op jit(solution)/shard_map/reduce_scatter | solution.py:199
  1066.4 16.9 %multiply_convert_fusion.3 = bf16[1024,1024]{0,1:T(8,128)(2,1)} fusion(f32[1024,1024]{0,1:T(8,128)} %copy-done.8, f32[1024]{0:T(1024)S(1)} %copy-done.52, bf16[1024,4608]{1,0:T(8,128)(2,1)} %get-tuple-element.67, bf16[4608,1024]{1,0:T(8,128)(2,1)} %all-gather.22.cloned.1.call-done), kind=kOutput, calls=%fused_computation.72 | convolution fusion | flops 9666822144 | bytes 25169920 | tf_op jit(solution)/shard_map/dot_general | solution.py:59
  1105.5 15.8 %all-reduce.4 = (bf16[256]{0:T(256)(128)(2,1)S(1)}, bf16[32]{0:T(256)(128)(2,1)S(1)}, bf16[256]{0:T(256)(128)(2,1)S(1)}) all-reduce(bf16[256]{0:T(256)(128)(2,1)S(1)} %dynamic-slice.2, bf16[32]{0:T(256)(128)(2,1)S(1)} %dynamic-slice.4, bf16[256]{0:T(256)(128)(2,1)S(1)} %dynamic-slice.6), channel_id=1, replica_groups=mesh['shard'=4,'rep'=8] {'rep'}, use_global_device_ids=true, to_apply=%region_17.18 | all-reduce | flops 544 | bytes 2176 | tf_op jit(solution)/shard_map/psum | solution.py:309
  1132.8 119.3 %all-reduce.9.cloned.1.call-done = (bf16[256,1024]{1,0:T(8,128)(2,1)}, bf16[256,512]{1,0:T(8,128)(2,1)}, bf16[256,512]{1,0:T(8,128)(2,1)}, bf16[256,1024]{1,0:T(...) async-done(((bf16[256,1024]{1,0:T(8,128)(2,1)}, bf16[256,512]{1,0:T(8,128)(2,1)}, bf16[256,512]{1,0:T(8,128)(2,1)}, ...) | async-done | bytes 8650768 | tf_op jit(solution)/shard_map/psum | solution.py:310
  (260 shorter events, 302.1 us)
Async XLA Ops:
  7.2 46.2 %all-gather.12.cloned.1.call-start = ((), (), s32[]{:S(2)}) async-start(), calls=%async_computation.8 | async-start | bytes 1310720 | tf_op jit(solution)/shard_map/all_gather | solution.py:97
  7.9 59.9 %all-gather.10.cloned.1.call-start = ((), (), s32[]{:S(2)}) async-start(), calls=%async_computation.7 | async-start | bytes 1310720 | tf_op jit(solution)/shard_map/all_gather | solution.py:98
  8.7 96.3 %all-gather.14.cloned.1.call-start = ((), (), s32[]{:S(2)}) async-start(), calls=%async_computation.9 | async-start | bytes 2621440 | tf_op jit(solution)/shard_map/all_gather | solution.py:96
  9.4 188.8 %all-gather.16.cloned.1.call-start = ((), (), s32[]{:S(2)}) async-start(), calls=%async_computation.10 | async-start | bytes 2621440 | tf_op jit(solution)/shard_map/all_gather | solution.py:100
  10.0 230.1 %all-gather.20.cloned.1.call-start = ((), (), s32[]{:S(2)}) async-start(), calls=%async_computation.12 | async-start | bytes 11796480 | tf_op jit(solution)/shard_map/all_gather | solution.py:155
  10.6 327.6 %all-gather.18.cloned.1.call-start = ((), (), s32[]{:S(2)}) async-start(), calls=%async_computation.11 | async-start | bytes 11796480 | tf_op jit(solution)/shard_map/all_gather | solution.py:154
  11.2 425.2 %all-gather.22.cloned.1.call-start = ((), (), s32[]{:S(2)}) async-start(), calls=%async_computation.13 | async-start | bytes 11796480 | tf_op jit(solution)/shard_map/all_gather | solution.py:156
  11.9 742.8 %reduce-scatter.12.cloned.1.call-start = ((), (), s32[]{:S(2)}) async-start(), calls=%async_computation.16 | async-start | bytes 1310720 | tf_op jit(solution)/shard_map/reduce_scatter | solution.py:287
  26.7 83.2 %copy-start.54 = (f32[64]{0:T(128)}, f32[64]{0:T(128)S(1)}, u32[]{:S(2)}) copy-start(f32[64]{0:T(128)S(1)} %get-tuple-element.103) | copy-start | bytes 772
  42.5 62.5 %copy-start.47 = (f32[4,1,256]{2,1,0:T(1,128)}, f32[4,1,256]{2,1,0:T(1,128)S(1)}, u32[]{:S(2)}) copy-start(f32[4,1,256]{2,1,0:T(1,128)S(1)} %convert_element_type.226) | copy-start | bytes 12292
  47.5 57.5 %copy-start.2 = (bf16[1024,1024]{0,1:T(8,128)(2,1)}, bf16[1024,1024]{0,1:T(8,128)(2,1)S(1)}, u32[]{:S(2)}) copy-start(bf16[1024,1024]{0,1:T(8,128)(2,1)S(1)} %copy.61) | copy-start | bytes 6291460
  53.3 57.7 %copy-start.24 = (f32[1024,32]{0,1:T(8,128)}, f32[1024,32]{0,1:T(8,128)S(1)}, u32[]{:S(2)}) copy-start(f32[1024,32]{0,1:T(8,128)S(1)} %get-tuple-element.94) | copy-start | bytes 393220
  53.3 57.7 %copy-start.26 = (f32[1024,32]{0,1:T(8,128)}, f32[1024,32]{0,1:T(8,128)S(1)}, u32[]{:S(2)}) copy-start(f32[1024,32]{0,1:T(8,128)S(1)} %get-tuple-element.95) | copy-start | bytes 393220
  58.3 96.5 %copy-start.10 = (bf16[1024,8,32]{0,2,1:T(8,128)(2,1)}, bf16[1024,8,32]{0,2,1:T(8,128)(2,1)S(1)}, u32[]{:S(2)}) copy-start(bf16[1024,8,32]{0,2,1:T(8,128)(2,1)S(1)} %get-tuple-element.80) | copy-start | bytes 1572868
  58.3 96.5 %copy-start.12 = (bf16[1024,8,32]{0,2,1:T(8,128)(2,1)}, bf16[1024,8,32]{0,2,1:T(8,128)(2,1)S(1)}, u32[]{:S(2)}) copy-start(bf16[1024,8,32]{0,2,1:T(8,128)(2,1)S(1)} %get-tuple-element.81) | copy-start | bytes 1572868
  256.3 180.1 %copy-start.18 = (bf16[1024,1024]{0,1:T(8,128)(2,1)S(1)}, bf16[1024,1024]{0,1:T(8,128)(2,1)}, u32[]{:S(2)}) copy-start(bf16[1024,1024]{0,1:T(8,128)(2,1)} %copy.65) | copy-start | bytes 6291460
  256.3 180.1 %copy-start.51 = (f32[1024]{0:T(1024)S(1)}, f32[1024]{0:T(1024)}, u32[]{:S(2)}) copy-start(f32[1024]{0:T(1024)} %compare_convert_fusion) | copy-start | bytes 12292
  579.9 174.9 %reduce-scatter.10.cloned.1.call-start = ((), (), s32[]{:S(2)}) async-start(), calls=%async_computation.15 | async-start | bytes 1310720 | tf_op jit(solution)/shard_map/reduce_scatter | solution.py:284
  666.6 88.2 %reduce-scatter.14.cloned.1.call-start = ((), (), s32[]{:S(2)}) async-start(), calls=%async_computation.17 | async-start | bytes 2621440 | tf_op jit(solution)/shard_map/reduce_scatter | solution.py:293
  673.4 98.8 %reduce-scatter.8.cloned.1.call-start = ((), (), s32[]{:S(2)}) async-start(), calls=%async_computation.14 | async-start | bytes 2621440 | tf_op jit(solution)/shard_map/reduce_scatter | solution.py:281
  702.7 167.5 %reduce-scatter.16.cloned.1.call-start = ((), (), s32[]{:S(2)}) async-start(), calls=%async_computation.18 | async-start | bytes 11796480 | tf_op jit(solution)/shard_map/reduce_scatter | solution.py:193
  719.6 248.7 %reduce-scatter.18.cloned.1.call-start = ((), (), s32[]{:S(2)}) async-start(), calls=%async_computation.19 | async-start | bytes 11796480 | tf_op jit(solution)/shard_map/reduce_scatter | solution.py:196
  736.0 330.4 %reduce-scatter.20.cloned.1.call-start = ((), (), s32[]{:S(2)}) async-start(), calls=%async_computation.20 | async-start | bytes 11796480 | tf_op jit(solution)/shard_map/reduce_scatter | solution.py:199
  753.2 499.0 %all-reduce.9.cloned.1.call-start = ((), (), s32[]{:S(2)}) async-start(), calls=%async_computation.21 | async-start | bytes 17301504 | tf_op jit(solution)/shard_map/psum | solution.py:310
  (56 other events, 564.4 us)
Sparse Core Ops, SparseCore 0:
  9.9 29.4 all-gather.11
  41.2 26.6 all-gather.9
  69.7 35.2 all-gather.13
  106.7 35.2 all-gather.15
  143.7 96.3 all-gather.19
  241.8 96.3 all-gather.17
  340.0 96.3 all-gather.21
  580.0 27.7 reduce-scatter.11
  666.7 28.3 reduce-scatter.9
  697.9 35.1 reduce-scatter.13
  736.9 35.1 reduce-scatter.7
  775.1 95.0 reduce-scatter.15
  873.3 94.9 reduce-scatter.17
  971.3 95.0 reduce-scatter.19
  1069.1 182.9 all-reduce.8
where the time goes:
time: 1280 us
  waiting for transfers between devices  676 us (53%)
  matrix products  379 us (30%)
  other arithmetic  125 us (10%)
  blocking collectives  51.4 us (4%)
  local copies, waits for them, and re-layouts  25.2 us (2%)
  between operations  17.1 us (1%)
    psum x1, waiting for transfers between devices, body(): lax.psum(share_query.astype(jnp.bfloat16), 'rep').astype(jnp.float32)  119 us
    reduce_scatter x1, waiting for transfers between devices, body(): lax.psum_scatter(grad_w_up.astype(jnp.bfloat16), 'shard', scatter_dimensi...  98.1 us
    reduce_scatter x1, waiting for transfers between devices, body(): lax.psum_scatter(grad_w_gate.astype(jnp.bfloat16), 'shard', scatter_dimen...  98 us
    reduce_scatter x1, waiting for transfers between devices, body(): lax.psum_scatter(grad_w_down.astype(jnp.bfloat16), 'shard', scatter_dimen...  98 us
    all_gather x1, waiting for transfers between devices, body(): lax.all_gather(w_gate, 'shard', axis=0, tiled=True)  81.8 us
    all_gather x1, waiting for transfers between devices, body(): lax.all_gather(w_down, 'shard', axis=0, tiled=True)  81.1 us
    dot_general x7, matrix products, matmul_cols(): lax.dot_general(left_mat, right_mat, (((1,), (1,)), ((), ())), preferred_...  73.2 us
    dot_general x7, matrix products, matmul_rows(): lax.dot_general(left_mat, right_mat, (((0,), (0,)), ((), ())), preferred_...  65.6 us
  transfers between devices with their start and end apart: 15, of which 10 were waited for; matrix products, arithmetic and copies ran while one was open for 28% of the time, Pallas kernels for 0%

commit v1 on v0

--- a/solution.py
+++ b/solution.py
@@ -9,6 +9,11 @@
 HD = 64
 norm_eps = 1e-05
 rope_base = 1000000.0
+
+
+def unite_knots(raw):
+    long_array = jax.lax.all_gather(raw, "rep")
+    return jnp.sum(long_array, axis=0)
 
 
 def inv_rms(values):
@@ -307,7 +312,7 @@
         share_down,
     ) = (
         lax.psum(share_again.astype(jnp.bfloat16), "rep").astype(jnp.float32),
-        lax.psum(share_query.astype(jnp.bfloat16), "rep").astype(jnp.float32),
+        unite_knots(share_query.astype(jnp.bfloat16)).astype(jnp.float32),
         lax.psum(share_key.astype(jnp.bfloat16), "rep").astype(jnp.float32),
         lax.psum(share_value.astype(jnp.bfloat16), "rep").astype(jnp.float32),
         lax.psum(share_qk.astype(jnp.bfloat16), "rep").astype(jnp.float32),

time: 1280 us -> 1320 us (1.031)
  waiting for transfers between devices: 676 us -> 710 us
    psum x1, waiting for transfers between devices: 119 us -> 152 us  [body(): lax.psum(share_key.astype(jnp.bfloat16), 'rep').astype(jnp.float32)]
    reduce_scatter x1, waiting for transfers between devices: 0.02 us -> 18 us  [body(): lax.psum_scatter(grad_w_out.astype(jnp.bfloat16), 'shard', scatter_dimens...]
    reduce_scatter x1, waiting for transfers between devices: 17.3 us -> 0.02 us  [body(): lax.psum_scatter(grad_w_query.astype(jnp.bfloat16), 'shard', scatter_dime...]
  transfers between devices with their start and end apart: 15 -> 16, of which waited for: 10 -> 10; matrix products, arithmetic and copies ran while one was open for 28% -> 24% of each run, Pallas kernels for 0% -> 0%
where the time goes in v1:
time: 1320 us
  waiting for transfers between devices  710 us (54%)
  matrix products  382 us (29%)
  other arithmetic  128 us (10%)
  blocking collectives  51.1 us (4%)
  local copies, waits for them, and re-layouts  27.8 us (2%)
  between operations  17.1 us (1%)
    psum x1, waiting for transfers between devices, body(): lax.psum(share_key.astype(jnp.bfloat16), 'rep').astype(jnp.float32)  152 us
    reduce_scatter x1, waiting for transfers between devices, body(): lax.psum_scatter(grad_w_up.astype(jnp.bfloat16), 'shard', scatter_dimensi...  98.1 us
    reduce_scatter x1, waiting for transfers between devices, body(): lax.psum_scatter(grad_w_down.astype(jnp.bfloat16), 'shard', scatter_dimen...  98 us
    reduce_scatter x1, waiting for transfers between devices, body(): lax.psum_scatter(grad_w_gate.astype(jnp.bfloat16), 'shard', scatter_dimen...  98 us
    all_gather x1, waiting for transfers between devices, body(): lax.all_gather(w_gate, 'shard', axis=0, tiled=True)  81.8 us
    all_gather x1, waiting for transfers between devices, body(): lax.all_gather(w_down, 'shard', axis=0, tiled=True)  81 us
    dot_general x7, matrix products, matmul_cols(): lax.dot_general(left_mat, right_mat, (((1,), (1,)), ((), ())), preferred_...  73.4 us
    dot_general x7, matrix products, matmul_rows(): lax.dot_general(left_mat, right_mat, (((0,), (0,)), ((), ())), preferred_...  65.6 us
  transfers between devices with their start and end apart: 16, of which 10 were waited for; matrix products, arithmetic and copies ran while one was open for 24% of the time, Pallas kernels for 0%

profile of v1, /device:TPU:0, one launch (start us, length us, event | category | flops | bytes accessed | tf_op | source)
XLA Modules:
  0.0 1316.8 jit_solution(3591209616796538809)
XLA Ops:
  71.4 33.6 %all-gather.16.cloned.1.call-done = bf16[1024,1024]{1,0:T(8,128)(2,1)} async-done(((bf16[256,1024]{1,0:T(8,128)(2,1)}), bf16[1024,1024]{1,0:T(8,128)(2,1)}) %all-gather.16.cloned.1.call-update) | async-done | bytes 2097168 | tf_op jit(solution)/shard_map/all_gather | solution.py:101
  181.8 16.5 %fusion.45 = bf16[8,64,2,512]{3,1,2,0:T(8,128)(2,1)} fusion(bf16[1024,8,64,1]{0,2,3,1:T(8,128)(2,1)S(1)} %bitcast.202, f32[8,2,512,1024]{2,3,1,0:T(8,128)} %get-tuple-element.110, f32[8,2,512]{2,1,0:T(2,128)S(1)} %fusion.6, f32[8,2,512]{2,1,0:T(2,128)S(1)} %get-tuple-element.109), kind=kOutput, calls=%fused_computation.116 | convolution fusion | flops 1099431936 | bytes 35717120 | tf_op jit(solution)/shard_map/grqk,kgd->qgrd/dot_general | solution.py:151
  205.6 34.5 %all-gather.22.cloned.1.call-done = bf16[1024,4608]{1,0:T(8,128)(2,1)} async-done(((bf16[256,4608]{1,0:T(8,128)(2,1)}), bf16[1024,4608]{1,0:T(8,128)(2,1)}) %all-gather.22.cloned.1.call-update) | async-done | bytes 9437200 | tf_op jit(solution)/shard_map/all_gather | solution.py:160
  240.1 16.2 %fusion.66 = f32[1024,4608]{1,0:T(8,128)} fusion(bf16[1024,1024]{0,1:T(8,128)(2,1)S(1)} %multiply_convert_fusion.4, bf16[1024,4608]{1,0:T(8,128)(2,1)} %all-gather.22.cloned.1.call-done), kind=kOutput, calls=%fused_computation.156 | convolution fusion | flops 9663676416 | bytes 30408704 | tf_op jit(solution)/shard_map/dot_general | solution.py:64
  256.3 81.8 %all-gather.20.cloned.1.call-done = bf16[1024,4608]{1,0:T(8,128)(2,1)} async-done(((bf16[256,4608]{1,0:T(8,128)(2,1)}), bf16[1024,4608]{1,0:T(8,128)(2,1)}) %all-gather.20.cloned.1.call-update) | async-done | bytes 9437200 | tf_op jit(solution)/shard_map/all_gather | solution.py:159
  338.2 17.2 %fusion.65 = f32[1024,4608]{1,0:T(8,128)} fusion(bf16[1024,1024]{0,1:T(8,128)(2,1)} %copy-done.33, bf16[1024,4608]{1,0:T(8,128)(2,1)} %all-gather.20.cloned.1.call-done), kind=kOutput, calls=%fused_computation.155 | convolution fusion | flops 9663676416 | bytes 30408704 | tf_op jit(solution)/shard_map/dot_general | solution.py:64
  355.4 81.0 %all-gather.24.cloned.1.call-done = bf16[4608,1024]{1,0:T(8,128)(2,1)} async-done(((bf16[1152,1024]{1,0:T(8,128)(2,1)}), bf16[4608,1024]{1,0:T(8,128)(2,1)}) %all-gather.24.cloned.1.call-update) | async-done | bytes 9437200 | tf_op jit(solution)/shard_map/all_gather | solution.py:161
  436.4 31.3 %multiply_convert_fusion = (bf16[1024,4608]{1,0:T(8,128)(2,1)}, bf16[1024,4608]{1,0:T(8,128)(2,1)}, bf16[1024,4608]{1,0:T(8,128)(2,1)}) fusion(f32[1024,4608]{1,0:T(8,128)} %fusion.65, f32[1024,4608]{1,0:T(8,128)} %fusion.66, bf16[4608,1024]{1,0:T(8,128)(2,1)} %all-gather.24.cloned.1.call-done, bf16[1024,1024]{0,1:T(8,128)(2,1)S(1)} %copy-done.19, ...), kind=kOutput, calls=%fused_computation.22 | convolution fusion | flops 9737601024 | bytes 77598720 | tf_op jit(solution)/shard_map/dot_general | solution.py:74
  482.3 16.5 %multiply_reduce_fusion = (bf16[1024]{0:T(1024)(128)(2,1)}, f32[1024]{0:T(1024)S(1)}, f32[1024,1024]{0,1:T(8,128)S(1)}) fusion(f32[1024,1024]{0,1:T(8,128)S(1)} %copy-done.9, f32[1024]{0:T(1024)S(1)} %get-tuple-element.98, f32[1024]{0:T(1024)S(1)} %bitcast.225, f32[1024,1024]{0,1:T(8,128)S(1)} %fusion.67, bf16[1024,4608]{1,0:T(8,128)(2,1)} %get-tuple-element.64, ...), kind=kOutput, calls=%fused_computation.65 | convolution fusion | flops 9671014400 | bytes 31471616 | tf_op jit(solution)/shard_map/dot_general | solution.py:74
  504.3 21.8 %fusion.3 = (f32[8,2,512]{2,1,0:T(2,128)S(1)}, f32[8,1024,512,2]{2,1,3,0:T(8,128)}) fusion(f32[8,2,512,1024]{2,3,1,0:T(8,128)} %get-tuple-element.110, f32[8,2,512]{2,1,0:T(2,128)S(1)} %bitcast.206, bf16[1024,8,64,1]{0,2,3,1:T(8,128)(2,1)S(1)} %bitcast.203, bf16[512,8,2,64]{0,3,2,1:T(8,128)(2,1)S(1)} %bitcast.191), kind=kOutput, calls=%fused_computation.7 | convolution fusion | flops 1098899456 | bytes 69271552 | tf_op jit(solution)/shard_map/qgrd,kgd->grqk/dot_general | solution.py:234
  526.2 27.6 %fusion.5 = bf16[8,2,512,1024]{2,3,1,0:T(8,128)(2,1)} fusion(f32[8,1024,512,2]{2,1,3,0:T(8,128)} %get-tuple-element.117, f32[8,2,512,1024]{2,3,1,0:T(8,128)} %get-tuple-element.110, f32[8,2,512]{2,1,0:T(2,128)S(1)} %get-tuple-element.116, f32[8,2,512]{2,1,0:T(2,128)S(1)} %bitcast.207), kind=kLoop, calls=%fused_computation.9 | loop fusion | flops 33554432 | bytes 83951616 | tf_op jit(solution)/shard_map/convert_element_type | solution.py:238
  564.0 22.0 %fusion = (f32[8,2,512]{2,1,0:T(2,128)S(1)}, f32[8,1024,512,2]{2,1,3,0:T(8,128)}) fusion(f32[8,2,512,1024]{2,3,1,0:T(8,128)} %get-tuple-element.108, f32[8,2,512]{2,1,0:T(2,128)S(1)} %bitcast.209, bf16[1024,8,64,1]{0,2,3,1:T(8,128)(2,1)S(1)} %bitcast.204, bf16[512,8,2,64]{0,3,2,1:T(8,128)(2,1)S(1)} %bitcast.193), kind=kOutput, calls=%fused_computation.2 | convolution fusion | flops 1098899456 | bytes 69271552 | tf_op jit(solution)/shard_map/qgrd,kgd->grqk/dot_general | solution.py:234
  586.0 27.4 %fusion.2 = bf16[8,2,512,1024]{2,3,1,0:T(8,128)(2,1)} fusion(f32[8,1024,512,2]{2,1,3,0:T(8,128)} %get-tuple-element.115, f32[8,2,512,1024]{2,3,1,0:T(8,128)} %get-tuple-element.108, f32[8,2,512]{2,1,0:T(2,128)S(1)} %get-tuple-element.114, f32[8,2,512]{2,1,0:T(2,128)S(1)} %bitcast.210), kind=kLoop, calls=%fused_computation.4 | loop fusion | flops 33554432 | bytes 83951616 | tf_op jit(solution)/shard_map/convert_element_type | solution.py:238
  634.8 15.5 %fusion.11 = f32[8,64,1024,1]{2,1,3,0:T(8,128)} fusion(bf16[512,8,2,64]{0,3,2,1:T(8,128)(2,1)} %bitcast.194, f32[8,2,512,1024]{2,3,1,0:T(8,128)} %get-tuple-element.108, f32[8,2,512]{2,1,0:T(2,128)S(1)} %bitcast.211), kind=kOutput, calls=%fused_computation.27 | convolution fusion | flops 1090519040 | bytes 36732928 | tf_op jit(solution)/shard_map/grqk,qgrd->kgd/dot_general | solution.py:246
  650.3 15.6 %fusion.36 = bf16[8,64,1024]{2,1,0:T(8,128)(2,1)} fusion(f32[8,64,1024,1]{2,1,3,0:T(8,128)} %fusion.11, bf16[512,8,2,64]{0,3,2,1:T(8,128)(2,1)S(1)} %bitcast.192, f32[8,2,512,1024]{2,3,1,0:T(8,128)} %get-tuple-element.110, f32[8,2,512]{2,1,0:T(2,128)S(1)} %bitcast.208), kind=kOutput, calls=%fused_computation.90 | convolution fusion | flops 1091567616 | bytes 37781504 | tf_op jit(solution)/shard_map/grqk,qgrd->kgd/dot_general | solution.py:246
  708.4 16.3 %convolution_convert_fusion.1 = bf16[1024,4608]{1,0:T(8,128)(2,1)} fusion(bf16[1024,1024]{0,1:T(8,128)(2,1)} %copy-done.33, bf16[1024,4608]{1,0:T(8,128)(2,1)} %get-tuple-element.65), kind=kOutput, calls=%fused_computation.34 | convolution fusion | flops 9668395008 | bytes 20971520 | tf_op jit(solution)/shard_map/dot_general | solution.py:68
  725.0 16.4 %convolution_convert_fusion = bf16[1024,4608]{1,0:T(8,128)(2,1)} fusion(bf16[1024,1024]{0,1:T(8,128)(2,1)} %copy-done.33, bf16[1024,4608]{1,0:T(8,128)(2,1)} %get-tuple-element.64), kind=kOutput, calls=%fused_computation.33 | convolution fusion | flops 9668395008 | bytes 20971520 | tf_op jit(solution)/shard_map/dot_general | solution.py:68
  742.1 16.6 %convolution_convert_fusion.2 = bf16[4608,1024]{1,0:T(8,128)(2,1)} fusion(bf16[1024,4608]{1,0:T(8,128)(2,1)} %get-tuple-element.66, bf16[1024,1024]{0,1:T(8,128)(2,1)} %copy.65, f32[1024]{0:T(1024)S(1)} %copy-done.54), kind=kOutput, calls=%fused_computation.35 | convolution fusion | flops 9671540736 | bytes 20975616 | tf_op jit(solution)/shard_map/dot_general | solution.py:68
  760.9 18.0 %reduce-scatter.14.cloned.1.call-done = bf16[256,1024]{1,0:T(8,128)(2,1)} async-done(((bf16[1024,1024]{1,0:T(8,128)(2,1)}), bf16[256,1024]{1,0:T(8,128)(2,1)}) %reduce-scatter.14.cloned.1.call-update) | async-done | bytes 524304 | tf_op jit(solution)/shard_map/reduce_scatter | solution.py:298
  778.9 98.0 %reduce-scatter.16.cloned.1.call-done = bf16[256,4608]{1,0:T(8,128)(2,1)} async-done(((bf16[1024,4608]{1,0:T(8,128)(2,1)}), bf16[256,4608]{1,0:T(8,128)(2,1)}) %reduce-scatter.16.cloned.1.call-update) | async-done | bytes 2359312 | tf_op jit(solution)/shard_map/reduce_scatter | solution.py:198
  876.9 98.1 %reduce-scatter.18.cloned.1.call-done = bf16[256,4608]{1,0:T(8,128)(2,1)} async-done(((bf16[1024,4608]{1,0:T(8,128)(2,1)}), bf16[256,4608]{1,0:T(8,128)(2,1)}) %reduce-scatter.18.cloned.1.call-update) | async-done | bytes 2359312 | tf_op jit(solution)/shard_map/reduce_scatter | solution.py:201
  975.1 98.0 %reduce-scatter.20.cloned.1.call-done = bf16[1152,1024]{1,0:T(8,128)(2,1)} async-done(((bf16[4608,1024]{1,0:T(8,128)(2,1)}), bf16[1152,1024]{1,0:T(8,128)(2,1)}) %reduce-scatter.20.cloned.1.call-update) | async-done | bytes 2359312 | tf_op jit(solution)/shard_map/reduce_scatter | solution.py:204
  1073.1 16.9 %multiply_convert_fusion.3 = bf16[1024,1024]{0,1:T(8,128)(2,1)} fusion(f32[1024,1024]{0,1:T(8,128)} %copy-done.8, f32[1024]{0:T(1024)S(1)} %copy-done.54, bf16[1024,4608]{1,0:T(8,128)(2,1)} %get-tuple-element.66, bf16[4608,1024]{1,0:T(8,128)(2,1)} %all-gather.24.cloned.1.call-done), kind=kOutput, calls=%fused_computation.72 | convolution fusion | flops 9666822144 | bytes 25169920 | tf_op jit(solution)/shard_map/dot_general | solution.py:64
  1143.4 152.4 %all-reduce.9.cloned.1.call-done = (bf16[256,512]{1,0:T(8,128)(2,1)}, bf16[256,512]{1,0:T(8,128)(2,1)}, bf16[256,1024]{1,0:T(8,128)(2,1)}, bf16[256,4608]{1,0:T(...) async-done(((bf16[256,512]{1,0:T(8,128)(2,1)}, bf16[256,512]{1,0:T(8,128)(2,1)}, bf16[256,1024]{1,0:T(8,128)(2,1)}, bf16[256,4608]{1,0:T(8,128)(2,1)}, ...) | async-done | bytes 8126480 | tf_op jit(solution)/shard_map/psum | solution.py:316
  (268 shorter events, 310.4 us)
Async XLA Ops:
  7.2 46.9 %all-gather.14.cloned.1.call-start = ((), (), s32[]{:S(2)}) async-start(), calls=%async_computation.8 | async-start | bytes 1310720 | tf_op jit(solution)/shard_map/all_gather | solution.py:102
  7.9 59.9 %all-gather.12.cloned.1.call-start = ((), (), s32[]{:S(2)}) async-start(), calls=%async_computation.7 | async-start | bytes 1310720 | tf_op jit(solution)/shard_map/all_gather | solution.py:103
  8.7 96.3 %all-gather.16.cloned.1.call-start = ((), (), s32[]{:S(2)}) async-start(), calls=%async_computation.9 | async-start | bytes 2621440 | tf_op jit(solution)/shard_map/all_gather | solution.py:101
  9.4 188.9 %all-gather.18.cloned.1.call-start = ((), (), s32[]{:S(2)}) async-start(), calls=%async_computation.10 | async-start | bytes 2621440 | tf_op jit(solution)/shard_map/all_gather | solution.py:105
  10.0 230.1 %all-gather.22.cloned.1.call-start = ((), (), s32[]{:S(2)}) async-start(), calls=%async_computation.12 | async-start | bytes 11796480 | tf_op jit(solution)/shard_map/all_gather | solution.py:160
  10.6 327.6 %all-gather.20.cloned.1.call-start = ((), (), s32[]{:S(2)}) async-start(), calls=%async_computation.11 | async-start | bytes 11796480 | tf_op jit(solution)/shard_map/all_gather | solution.py:159
  11.2 425.2 %all-gather.24.cloned.1.call-start = ((), (), s32[]{:S(2)}) async-start(), calls=%async_computation.13 | async-start | bytes 11796480 | tf_op jit(solution)/shard_map/all_gather | solution.py:161
  11.9 746.8 %reduce-scatter.8.cloned.1.call-start = ((), (), s32[]{:S(2)}) async-start(), calls=%async_computation.14 | async-start | bytes 2621440 | tf_op jit(solution)/shard_map/reduce_scatter | solution.py:286
  26.7 83.2 %copy-start.58 = (f32[64]{0:T(128)}, f32[64]{0:T(128)S(1)}, u32[]{:S(2)}) copy-start(f32[64]{0:T(128)S(1)} %get-tuple-element.102) | copy-start | bytes 772
  42.5 62.5 %copy-start.47 = (f32[4,1,256]{2,1,0:T(1,128)}, f32[4,1,256]{2,1,0:T(1,128)S(1)}, u32[]{:S(2)}) copy-start(f32[4,1,256]{2,1,0:T(1,128)S(1)} %convert_element_type.228) | copy-start | bytes 12292
  54.1 56.9 %copy-start.26 = (f32[1024,32]{0,1:T(8,128)}, f32[1024,32]{0,1:T(8,128)S(1)}, u32[]{:S(2)}) copy-start(f32[1024,32]{0,1:T(8,128)S(1)} %get-tuple-element.93) | copy-start | bytes 393220
  59.0 96.1 %copy-start.10 = (bf16[1024,8,32]{0,2,1:T(8,128)(2,1)}, bf16[1024,8,32]{0,2,1:T(8,128)(2,1)S(1)}, u32[]{:S(2)}) copy-start(bf16[1024,8,32]{0,2,1:T(8,128)(2,1)S(1)} %get-tuple-element.79) | copy-start | bytes 1572868
  59.0 96.0 %copy-start.12 = (bf16[1024,8,32]{0,2,1:T(8,128)(2,1)}, bf16[1024,8,32]{0,2,1:T(8,128)(2,1)S(1)}, u32[]{:S(2)}) copy-start(bf16[1024,8,32]{0,2,1:T(8,128)(2,1)S(1)} %get-tuple-element.80) | copy-start | bytes 1572868
  256.3 180.1 %copy-start.19 = (bf16[1024,1024]{0,1:T(8,128)(2,1)S(1)}, bf16[1024,1024]{0,1:T(8,128)(2,1)}, u32[]{:S(2)}) copy-start(bf16[1024,1024]{0,1:T(8,128)(2,1)} %copy.65) | copy-start | bytes 6291460
  256.3 180.1 %copy-start.53 = (f32[1024]{0:T(1024)S(1)}, f32[1024]{0:T(1024)}, u32[]{:S(2)}) copy-start(f32[1024]{0:T(1024)} %compare_convert_fusion) | copy-start | bytes 12292
  503.0 61.0 %copy-start.14 = (bf16[512,1024]{0,1:T(8,128)(2,1)}, bf16[512,1024]{0,1:T(8,128)(2,1)S(1)}, u32[]{:S(2)}) copy-start(bf16[512,1024]{0,1:T(8,128)(2,1)S(1)} %get-tuple-element.84) | copy-start | bytes 3145732
  634.7 126.1 %reduce-scatter.12.cloned.1.call-start = ((), (), s32[]{:S(2)}) async-start(), calls=%async_computation.16 | async-start | bytes 1310720 | tf_op jit(solution)/shard_map/reduce_scatter | solution.py:292
  681.7 79.1 %reduce-scatter.10.cloned.1.call-start = ((), (), s32[]{:S(2)}) async-start(), calls=%async_computation.15 | async-start | bytes 1310720 | tf_op jit(solution)/shard_map/reduce_scatter | solution.py:289
  701.6 77.3 %reduce-scatter.14.cloned.1.call-start = ((), (), s32[]{:S(2)}) async-start(), calls=%async_computation.17 | async-start | bytes 2621440 | tf_op jit(solution)/shard_map/reduce_scatter | solution.py:298
  708.4 168.5 %reduce-scatter.16.cloned.1.call-start = ((), (), s32[]{:S(2)}) async-start(), calls=%async_computation.18 | async-start | bytes 11796480 | tf_op jit(solution)/shard_map/reduce_scatter | solution.py:198
  724.8 250.3 %reduce-scatter.18.cloned.1.call-start = ((), (), s32[]{:S(2)}) async-start(), calls=%async_computation.19 | async-start | bytes 11796480 | tf_op jit(solution)/shard_map/reduce_scatter | solution.py:201
  741.4 331.7 %reduce-scatter.20.cloned.1.call-start = ((), (), s32[]{:S(2)}) async-start(), calls=%async_computation.20 | async-start | bytes 11796480 | tf_op jit(solution)/shard_map/reduce_scatter | solution.py:204
  758.7 380.5 %all-gather.26.cloned.1.call-start = ((), (), s32[]{:S(2)}) async-start(), calls=%async_computation.21 | async-start | bytes 4718592 | tf_op jit(solution)/shard_map/all_gather | solution.py:15
  759.2 536.5 %all-reduce.9.cloned.1.call-start = ((), (), s32[]{:S(2)}) async-start(), calls=%async_computation.22 | async-start | bytes 16252928 | tf_op jit(solution)/shard_map/psum | solution.py:316
  (59 other events, 600.6 us)
Sparse Core Ops, SparseCore 0:
  9.9 29.4 all-gather.13
  41.2 26.6 all-gather.11
  69.7 35.2 all-gather.15
  106.7 35.2 all-gather.17
  143.7 96.3 all-gather.21
  241.8 96.3 all-gather.19
  340.0 96.3 all-gather.23
  634.8 35.1 reduce-scatter.7
  681.9 27.4 reduce-scatter.11
  712.1 27.7 reduce-scatter.9
  743.7 35.1 reduce-scatter.13
  781.8 95.0 reduce-scatter.15
  880.0 95.0 reduce-scatter.17
  978.0 95.0 reduce-scatter.19
  1074.5 47.2 all-gather.25
  1124.6 171.1 all-reduce.8
